TPU v7x, 128 devices: a whole 4x4x4 slice. The times are simulated.
128 devices in a mesh: dp: 2 (over core), context: 2 (over y_lo), expert: 32 (over z, x, y_hi).
Axes of the slice: x: 4, y: 4 (y_hi: 2, y_lo: 2; y = y_hi * 2 + y_lo), z: 4, core: 2. Of those that a mesh axis runs over, the one named last changes fastest.
Arguments:
- tokens: bfloat16 [64, 256, 2048], P(('dp', 'expert'), 'context'), may hold values from -16 to 16
- grad_output: bfloat16 [64, 256, 2048], P(('dp', 'expert'), 'context'), may hold values from -6 to 6
- routes: int32 [64, 256, 8], P(('dp', 'expert'), 'context'), may hold values from 0 to 31, all different within a row; in each aligned block of 128 rows (0 to 127, 128 to 255, ..., all dimensions but the last counted through in order) at most 40 rows name the same one
- positions: int32 [64, 256], P(('dp', 'expert')), may hold values from 0 to 255, as said below
- attn_gain: float32 [2048], replicated, may hold values from 0.5 to 1.5
- q_gain: float32 [2048], replicated, may hold values from 0.1 to 1.9
- k_gain: float32 [2048], replicated, may hold values from 0.1 to 1.9
- ffn_gain: float32 [2048], replicated, may hold values from 0.5 to 1.5
- qkv_weight: bfloat16 [3, 2048, 2048], P(None, ('dp', 'context', 'expert')), may hold values from -0.125 to 0.125
- out_weight: bfloat16 [2048, 2048], P(('dp', 'context', 'expert')), may hold values from -1 to 1
- router_weight: bfloat16 [2048, 32], replicated, may hold values from -0.25 to 0.25
- expert_in: bfloat16 [32, 2, 2048, 1024], P('expert'), may hold values from -0.125 to 0.125
- expert_out: bfloat16 [32, 1024, 2048], P('expert'), may hold values from -0.75 to 0.75
Outputs:
- output: float32 [64, 256, 2048], P(('dp', 'expert'), 'context')
- grad_tokens: float32 [64, 256, 2048], P(('dp', 'expert'), 'context')
- grad_attn_gain: float32 [2048], replicated
- grad_q_gain: float32 [2048], replicated
- grad_k_gain: float32 [2048], replicated
- grad_ffn_gain: float32 [2048], replicated
- grad_router: float32 [2048, 32], replicated
- grad_qkv_weight: float32 [3, 2048, 2048], P(None, ('dp', 'context', 'expert'))
- grad_out_weight: float32 [2048, 2048], P(('dp', 'context', 'expert'))
- grad_expert_in: float32 [32, 2, 2048, 1024], P('expert', None, ('dp', 'context'))
- grad_expert_out: float32 [32, 1024, 2048], P('expert', None, ('dp', 'context'))
Inputs may be any that keep to these rules, and one draw needn't show every extreme that they name: `routes`: each row names 8 different experts; the rows of one device name one expert at most 40 times. Each row is a permutation of the positions of one sequence.
All inputs are finite; a program needn't handle non-finite values.
Results may differ from a plain program's by a relative error of at most 0.019.
Values may be sent and summed in bfloat16 or wider, within the bound.
No kernel may reach another device: no remote copies, remote signals or barrier semaphores. Data moves between devices by JAX's collectives and lax.ppermute only.
A program may use at most 448 MiB of HBM per device.

v0:
```python
import jax
import jax.numpy as jnp
from jax import lax
from jax.sharding import PartitionSpec as P

HDIM = 128
EPS = 1e-05
THETA = 10000.0


def rope_tables(places, head_dim):
    half = head_dim // 2
    freq = THETA ** (-jnp.arange(half, dtype=jnp.float32) * 2.0 / head_dim)
    angle = places.astype(jnp.float32)[:, None] * freq[None, :]
    return (jnp.cos(angle), jnp.sin(angle))


def rotate(values, cosine, sine, sign):
    half = values.shape[-1] // 2
    first = values[..., :half]
    second = values[..., half:]
    cosine = cosine[:, None, :]
    sine = sign * sine[:, None, :]
    return jnp.concatenate(
        [first * cosine - second * sine, second * cosine + first * sine], axis=-1
    )


def rms_forward(values):
    factor = lax.rsqrt(jnp.mean(values * values, axis=-1, keepdims=True) + EPS)
    return (values * factor, factor)


def rms_backward(grad_out, normed, factor, gain):
    scaled = grad_out * gain
    grad_in = factor * (scaled - normed * jnp.mean(scaled * normed, axis=-1, keepdims=True))
    return (grad_in, jnp.sum(grad_out * normed, axis=0))


def slot_index(route_rows, experts, capacity):
    onehot = (route_rows[:, None] == jnp.arange(experts, dtype=jnp.int32)[None, :]).astype(
        jnp.int32
    )
    count = route_rows.shape[0]
    earlier = (
        jnp.arange(count, dtype=jnp.int32)[None, :] < jnp.arange(count, dtype=jnp.int32)[:, None]
    ).astype(jnp.bfloat16)
    before = jnp.dot(earlier, onehot.astype(jnp.bfloat16), preferred_element_type=jnp.float32)
    return route_rows * capacity + jnp.sum(before.astype(jnp.int32) * onehot, axis=1)


def expert_major(received, local_experts, capacity):
    sources, _, width = received.shape
    return (
        received.reshape(sources, local_experts, capacity, width)
        .transpose(1, 0, 2, 3)
        .reshape(local_experts, sources * capacity, width)
    )


def source_major(results, sources, capacity):
    local_experts, _, width = results.shape
    return (
        results.reshape(local_experts, sources, capacity, width)
        .transpose(1, 0, 2, 3)
        .reshape(sources, local_experts * capacity, width)
    )


def swap_context(values):
    return lax.ppermute(values, "context", [(0, 1), (1, 0)])


def gather_context(values):
    other = swap_context(values)
    first = lax.axis_index("context") == 0
    return jnp.concatenate(
        [jnp.where(first, values, other), jnp.where(first, other, values)], axis=0
    )


def sum_context_halves(values):
    half = values.shape[0] // 2
    first = lax.axis_index("context") == 0
    own = jnp.where(first, values[:half], values[half:])
    given = jnp.where(first, values[half:], values[:half]).astype(jnp.bfloat16)
    return own + swap_context(given).astype(own.dtype)


def butterfly_sum(values, axes):
    index = lax.axis_index(axes)
    count = 1
    for name in axes:
        count *= lax.axis_size(name)
    step = 1
    while step < count:
        partner = [(i, i ^ step) for i in range(count)]
        received = lax.ppermute(values, axes, partner)
        mine_first = index & step == 0
        values = jnp.where(mine_first, values + received, received + values)
        step *= 2
    return values


def body(
    tokens,
    grad_output,
    routes,
    positions,
    attn_gain,
    q_gain,
    k_gain,
    ffn_gain,
    qkv_weight,
    out_weight,
    router_weight,
    expert_in,
    expert_out,
):
    single_precision = jnp.float32
    bf16 = jnp.bfloat16
    seq_tok = tokens.shape[1]
    width = tokens.shape[2]
    top = routes.shape[2]
    heads_width = out_weight.shape[1]
    head_dim = HDIM
    heads = heads_width // head_dim
    local_experts = expert_in.shape[0]
    experts = router_weight.shape[1]
    sources = lax.axis_size("expert")
    capacity = min(seq_tok, seq_tok * top * 5 // (4 * experts))
    scale = head_dim ** (-0.5)
    x = tokens[0].astype(single_precision)
    normed1, factor1 = rms_forward(x)
    attention_input = (normed1 * attn_gain).astype(bf16)
    all_axes = ("dp", "context", "expert")
    weights_full = lax.all_gather(
        jnp.concatenate([qkv_weight.transpose(1, 0, 2), out_weight[:, None, :]], axis=1),
        all_axes,
        axis=0,
        tiled=True,
    )
    out_full = weights_full[:, 3, :]
    projected_all = jnp.dot(
        attention_input,
        weights_full.reshape(width, 4 * heads_width),
        preferred_element_type=single_precision,
    ).reshape(seq_tok, 4, heads_width)
    projected_output = projected_all[:, :3].transpose(1, 0, 2)
    q_normed, q_factor = rms_forward(projected_output[0])
    k_normed, k_factor = rms_forward(projected_output[1])
    values = projected_output[2].astype(bf16)
    all_places = positions[0]
    own_places = lax.dynamic_slice_in_dim(all_places, lax.axis_index("context") * seq_tok, seq_tok)
    cosine, sine = rope_tables(own_places, head_dim)
    queries = rotate(
        (q_normed * q_gain).reshape(seq_tok, heads, head_dim), cosine, sine, 1.0
    ).astype(bf16)
    own_keys = rotate(
        (k_normed * k_gain).reshape(seq_tok, heads, head_dim), cosine, sine, 1.0
    ).astype(bf16)
    keys_vals = gather_context(jnp.stack([own_keys.reshape(seq_tok, heads_width), values], axis=1))
    keys = keys_vals[:, 0]
    vals = keys_vals[:, 1]
    seq_len = keys.shape[0]
    keys3 = keys.reshape(seq_len, heads, head_dim)
    vals3 = vals.reshape(seq_len, heads, head_dim)
    allowed = (all_places[None, :] <= own_places[:, None])[None]

    def masked_scores():
        scores = (
            jnp.einsum("qhd,khd->hqk", queries, keys3, preferred_element_type=single_precision)
            * scale
        )
        return jnp.where(allowed, scores, -jnp.inf)

    scores = masked_scores()
    lse = jnp.log(jnp.sum(jnp.exp(scores), axis=-1, keepdims=True))
    probs_b = jnp.exp(scores - lse).astype(bf16)
    attended = (
        jnp.einsum("hqk,khd->qhd", probs_b, vals3, preferred_element_type=single_precision)
        .astype(bf16)
        .reshape(seq_tok, heads_width)
    )
    mid = x + jnp.einsum("tq,dq->td", attended, out_full, preferred_element_type=single_precision)
    normed2, factor2 = rms_forward(mid)
    ffn_in = (normed2 * ffn_gain).astype(bf16)
    router_exp = jnp.exp(jnp.dot(ffn_in, router_weight, preferred_element_type=single_precision))
    router_probs = router_exp / jnp.sum(router_exp, axis=-1, keepdims=True)
    own_routes = routes[0]
    slots = slot_index(own_routes.reshape(-1), experts, capacity)
    send = (
        jnp.zeros((experts * capacity, width), bf16).at[slots].set(jnp.repeat(ffn_in, top, axis=0))
    )
    received = lax.all_to_all(
        send.reshape(sources, local_experts * capacity, width),
        "expert",
        split_axis=0,
        concat_axis=0,
        tiled=True,
    )
    rows = expert_major(received, local_experts, capacity)
    gate_up = jnp.einsum("lrd,lkdh->lkrh", rows, expert_in, preferred_element_type=single_precision)
    gate = gate_up[:, 0]
    up = gate_up[:, 1]
    sig = jax.nn.sigmoid(gate)
    hidden = (gate * sig * up).astype(bf16)
    results = jnp.einsum(
        "lrh,lhd->lrd", hidden, expert_out, preferred_element_type=single_precision
    ).astype(bf16)
    back = lax.all_to_all(
        source_major(results, sources, capacity), "expert", split_axis=0, concat_axis=0, tiled=True
    )
    route_out = back.reshape(experts * capacity, width)[slots].reshape(seq_tok, top, width)
    route_weight = jnp.take_along_axis(router_probs, own_routes, axis=1)
    output = mid + jnp.sum(route_weight[:, :, None] * route_out, axis=1)
    grad = grad_output[0].astype(single_precision)
    route_grad_weight = jnp.sum(grad[:, None, :] * route_out, axis=-1)
    route_grad = (
        (route_weight[:, :, None] * grad[:, None, :]).astype(bf16).reshape(seq_tok * top, width)
    )
    grad_send = jnp.zeros((experts * capacity, width), bf16).at[slots].set(route_grad)
    grad_received = lax.all_to_all(
        grad_send.reshape(sources, local_experts * capacity, width),
        "expert",
        split_axis=0,
        concat_axis=0,
        tiled=True,
    )
    grad_rows = expert_major(grad_received, local_experts, capacity)
    grad_hidden = jnp.einsum(
        "lrd,lhd->lrh", grad_rows, expert_out, preferred_element_type=single_precision
    )
    grad_down = jnp.einsum(
        "lrh,lrd->lhd", hidden, grad_rows, preferred_element_type=single_precision
    )
    grad_gate = (grad_hidden * up * sig * (1.0 + gate * (1.0 - sig))).astype(bf16)
    grad_up = (grad_hidden * gate * sig).astype(bf16)
    grad_gate_up = jnp.stack([grad_gate, grad_up], axis=1)
    grad_gate_up_w = jnp.einsum(
        "lrd,lkrh->lkdh", rows, grad_gate_up, preferred_element_type=single_precision
    )
    grad_rows_in = jnp.einsum(
        "lkrh,lkdh->lrd", grad_gate_up, expert_in, preferred_element_type=single_precision
    ).astype(bf16)
    grad_back = lax.all_to_all(
        source_major(grad_rows_in, sources, capacity),
        "expert",
        split_axis=0,
        concat_axis=0,
        tiled=True,
    )
    grad_route_in = grad_back.reshape(experts * capacity, width)[slots].reshape(seq_tok, top, width)
    grad_ffn_in = jnp.sum(grad_route_in, axis=1, dtype=single_precision)
    chosen = (own_routes[:, :, None] == jnp.arange(experts, dtype=jnp.int32)[None, None, :]).astype(
        single_precision
    )
    grad_probs = jnp.sum(route_grad_weight[:, :, None] * chosen, axis=1)
    grad_logits = (
        router_probs * (grad_probs - jnp.sum(router_probs * grad_probs, axis=-1, keepdims=True))
    ).astype(bf16)
    grad_router = jnp.einsum(
        "td,te->de", ffn_in, grad_logits, preferred_element_type=single_precision
    )
    grad_ffn_in = grad_ffn_in + jnp.einsum(
        "te,de->td", grad_logits, router_weight, preferred_element_type=single_precision
    )
    grad_mid_norm, grad_ffn_gain = rms_backward(grad_ffn_in, normed2, factor2, ffn_gain)
    grad_mid = grad + grad_mid_norm
    grad_mid_b = grad_mid.astype(bf16)
    grad_att = (
        jnp.einsum("td,dq->tq", grad_mid_b, out_full, preferred_element_type=single_precision)
        .astype(bf16)
        .reshape(seq_tok, heads, head_dim)
    )
    delta = jnp.sum(
        grad_att.astype(single_precision)
        * attended.reshape(seq_tok, heads, head_dim).astype(single_precision),
        axis=-1,
    )
    probs = jnp.exp(masked_scores() - lse)
    grad_vals = jnp.einsum(
        "hqk,qhd->khd", probs.astype(bf16), grad_att, preferred_element_type=single_precision
    )
    grad_p = jnp.einsum("qhd,khd->hqk", grad_att, vals3, preferred_element_type=single_precision)
    grad_scores = (probs * (grad_p - delta.T[:, :, None])).astype(bf16)
    grad_queries = (
        jnp.einsum("hqk,khd->qhd", grad_scores, keys3, preferred_element_type=single_precision)
        * scale
    )
    grad_keys_all = (
        jnp.einsum("hqk,qhd->khd", grad_scores, queries, preferred_element_type=single_precision)
        * scale
    )
    grad_keys_values = sum_context_halves(
        jnp.stack(
            [grad_keys_all.reshape(seq_len, heads_width), grad_vals.reshape(seq_len, heads_width)],
            axis=1,
        )
    )
    grad_keys = grad_keys_values[:, 0]
    grad_values = grad_keys_values[:, 1]
    grad_qn = rotate(grad_queries, cosine, sine, -1.0).reshape(seq_tok, heads_width)
    grad_kn = rotate(grad_keys.reshape(seq_tok, heads, head_dim), cosine, sine, -1.0).reshape(
        seq_tok, heads_width
    )
    grad_q_raw, grad_q_gain = rms_backward(grad_qn, q_normed, q_factor, q_gain)
    grad_k_raw, grad_k_gain = rms_backward(grad_kn, k_normed, k_factor, k_gain)
    projected_gradient = jnp.stack(
        [grad_q_raw, grad_k_raw, grad_values, jnp.zeros_like(grad_values)], axis=1
    ).astype(bf16)
    attention_input_gradient = jnp.dot(
        projected_gradient.reshape(seq_tok, 4 * heads_width),
        weights_full.reshape(width, 4 * heads_width).T,
        preferred_element_type=single_precision,
    )
    grad_x_norm, grad_attn_gain = rms_backward(
        attention_input_gradient, normed1, factor1, attn_gain
    )
    grad_tokens = grad_mid + grad_x_norm

    def scatter_over_copies(values):
        values = lax.psum_scatter(values.astype(bf16), "dp", scatter_dimension=1, tiled=True)
        values = lax.psum_scatter(values, "context", scatter_dimension=1, tiled=True)
        return values.astype(single_precision)

    grad_in_shard = scatter_over_copies(grad_gate_up_w[0])[None]
    grad_down_shard = scatter_over_copies(grad_down[0])[None]
    left = jnp.stack([attention_input] * 3 + [grad_mid_b])
    right = jnp.concatenate([projected_gradient[:, :3].transpose(1, 0, 2), attended[None]], axis=0)
    stacked = jnp.einsum("sta,stb->sab", left, right, preferred_element_type=single_precision)
    summed = lax.psum(stacked.astype(bf16), all_axes)
    shard_rows = width // lax.axis_size(all_axes)
    start = lax.axis_index(all_axes) * shard_rows
    weight_shard = lax.dynamic_slice_in_dim(summed, start, shard_rows, axis=1).astype(
        single_precision
    )
    grad_qkv_shard = weight_shard[:3]
    grad_out_shard = weight_shard[3]
    small_sum = butterfly_sum(
        jnp.concatenate(
            [grad_attn_gain, grad_q_gain, grad_k_gain, grad_ffn_gain, grad_router.reshape(-1)]
        ),
        all_axes,
    )
    sizes = [width, heads_width, heads_width, width, width * experts]
    offsets = [sum(sizes[:n]) for n in range(len(sizes))]
    totals = [small_sum[o : o + n] for o, n in zip(offsets, sizes)]
    totals[4] = totals[4].reshape(width, experts)
    return (
        output[None],
        grad_tokens[None],
        totals[0],
        totals[1],
        totals[2],
        totals[3],
        totals[4],
        grad_qkv_shard,
        grad_out_shard,
        grad_in_shard,
        grad_down_shard,
    )


def solution(mesh):
    return jax.shard_map(
        body,
        mesh=mesh,
        in_specs=(
            P(("dp", "expert"), "context", None),
            P(("dp", "expert"), "context", None),
            P(("dp", "expert"), "context", None),
            P(("dp", "expert"), None),
            P(),
            P(),
            P(),
            P(),
            P(None, ("dp", "context", "expert"), None),
            P(("dp", "context", "expert"), None),
            P(),
            P("expert", None, None, None),
            P("expert", None, None),
        ),
        out_specs=(
            P(("dp", "expert"), "context", None),
            P(("dp", "expert"), "context", None),
            P(),
            P(),
            P(),
            P(),
            P(),
            P(None, ("dp", "context", "expert"), None),
            P(("dp", "context", "expert"), None),
            P("expert", None, ("dp", "context"), None),
            P("expert", None, ("dp", "context")),
        ),
        check_vma=False,
    )
```

profile of v0, /device:TPU:1, one launch (start us, length us, event | category | flops | bytes accessed | tf_op | source)
XLA Modules:
  0.0 1209.6 jit_solution(8714754060576962103)
XLA Ops:
  13.1 237.4 %all-gather.2.cloned.1.call-done = bf16[2048,4,2048]{2,0,1:T(8,128)(2,1)} async-done(((bf16[16,4,2048]{2,0,1:T(8,128)(2,1)}), bf16[2048,4,2048]{2,0,1:T(8,128)(2,1)}) %all-gather.2.cloned.1.call-update) | async-done | bytes 33554448 | tf_op jit(solution)/shard_map/all_gather | solution.py:137
  250.6 42.7 %copy.110 = bf16[2048,4,2048]{0,2,1:T(8,128)(2,1)} copy(bf16[2048,4,2048]{2,0,1:T(8,128)(2,1)} %all-gather.2.cloned.1.call-done) | data formatting | bytes 67108864 | tf_op jit(solution)/shard_map/all_gather | solution.py:137
  293.3 17.2 %fusion.33 = f32[3,128,2048]{2,1,0:T(8,128)S(1)} fusion(bf16[2048,4,2048]{0,2,1:T(8,128)(2,1)} %copy.110, bf16[1,128,2048]{2,1,0:T(8,128)(2,1)S(1)} %fusion.83), kind=kOutput, calls=%fused_computation.54 | convolution fusion | flops 3221225472 | bytes 37224448 | tf_op jit(solution)/shard_map/slice | solution.py:149
  317.9 21.8 %collective-permute-done = bf16[128,2,2048]{2,0,1:T(8,128)(2,1)S(1)} collective-permute-done((bf16[128,2,2048]{2,0,1:T(8,128)(2,1)}, bf16[128,2,2048]{2,0,1:T(8,128)(2,1)S(1)}, u32[]{:S(2)}, u32[]{:S(2)}) %collective-permute-start) | collective-permute-done | bytes 1048608 | tf_op jit(solution)/shard_map/ppermute | solution.py:71
  381.5 10.0 scatter_custom_fusion.1
  391.5 49.0 %all-to-all-done = bf16[32,40,2048]{2,1,0:T(8,128)(2,1)} async-done(((bf16[32,40,2048]{2,1,0:T(8,128)(2,1)}), bf16[32,40,2048]{2,1,0:T(8,128)(2,1)}, u32[]{:S(2)}, u32[]{:S(2)}) %all-to-all-start) | async-done | bytes 5242912 | tf_op jit(solution)/shard_map/all_to_all | solution.py:195
  447.4 16.8 %fusion.11 = f32[1,2,1280,1024]{3,2,1,0:T(8,128)S(1)} fusion(bf16[1280,2048,1]{1,0,2:T(8,128)(2,1)} %bitcast.24, bf16[1,2,2048,1024]{3,2,1,0:T(8,128)(2,1)} %param.24), kind=kOutput, calls=%fused_computation.25 | convolution fusion | flops 10737418240 | bytes 24117248 | tf_op jit(solution)/shard_map/lrd,lkdh->lkrh/dot_general | solution.py:203
  470.9 42.7 %all-to-all-done.2 = bf16[32,40,2048]{2,1,0:T(8,128)(2,1)} async-done(((bf16[32,40,2048]{2,1,0:T(8,128)(2,1)}), bf16[32,40,2048]{2,1,0:T(8,128)(2,1)}, u32[]{:S(2)}, u32[]{:S(2)}) %all-to-all-start.2) | async-done | bytes 5242912 | tf_op jit(solution)/shard_map/all_to_all | solution.py:223
  513.6 10.1 convolution_convert_fusion.2
  524.3 13.1 %fusion.41 = (bf16[1,1,1280,1024]{3,2,1,0:T(8,128)(2,1)S(1)}, bf16[1,1,1280,1024]{3,2,1,0:T(8,128)(2,1)S(1)}) fusion(f32[1,2,1280,1024]{3,2,1,0:T(8,128)} %copy-done.5, bf16[1280,2048]{1,0:T(8,128)(2,1)} %bitcast.41, bf16[1,1024,2048]{2,1,0:T(8,128)(2,1)} %param.25), kind=kOutput, calls=%fused_computation.60 | convolution fusion | flops 5385748480 | bytes 25165824 | tf_op jit(solution)/shard_map/lrd,lhd->lrh/dot_general | solution.py:231
  539.7 16.1 %convert_bitcast_fusion = bf16[2,2048,1024]{1,2,0:T(8,128)(2,1)} fusion(bf16[1280,2048,1]{1,0,2:T(8,128)(2,1)} %bitcast.24, bf16[1,1,1280,1024]{3,2,1,0:T(8,128)(2,1)S(1)} %get-tuple-element.74, bf16[1,1,1280,1024]{3,2,1,0:T(8,128)(2,1)S(1)} %get-tuple-element.73), kind=kOutput, calls=%fused_computation.21 | convolution fusion | flops 10744233984 | bytes 18874368 | tf_op jit(solution)/shard_map/lrd,lkrh->lkdh/dot_general | solution.py:240
  574.5 18.7 %bitcast_convert_fusion = bf16[1280,2048]{1,0:T(8,128)(2,1)} fusion(bf16[1,2,2048,1024]{3,2,1,0:T(8,128)(2,1)} %param.24, bf16[1,1,1280,1024]{3,2,1,0:T(8,128)(2,1)} %copy-done.64, bf16[1,1,1280,1024]{3,2,1,0:T(8,128)(2,1)} %copy-done.63), kind=kOutput, calls=%fused_computation.11 | convolution fusion | flops 10742661120 | bytes 18874368 | tf_op jit(solution)/shard_map/lkrh,lkdh->lrd/dot_general | solution.py:243
  593.2 46.6 %all-to-all-done.1 = bf16[32,40,2048]{2,1,0:T(8,128)(2,1)} async-done(((bf16[32,40,2048]{2,1,0:T(8,128)(2,1)}), bf16[32,40,2048]{2,1,0:T(8,128)(2,1)}, u32[]{:S(2)}, u32[]{:S(2)}) %all-to-all-start.1) | async-done | bytes 5242912 | tf_op jit(solution)/shard_map/all_to_all | solution.py:211
  639.9 11.2 all-to-all-start.3
  653.5 12.2 %gather_fusion = bf16[1024,2048]{1,0:T(8,128)(2,1)} fusion(bf16[1280,2048]{1,0:T(8,128)(2,1)} %bitcast.34, s32[1024]{0:T(1024)S(1)} %broadcast_clamp_fusion), kind=kCustom, calls=%fused_computation | custom fusion | bytes 8392704 | tf_op jit(solution)/shard_map/gather | solution.py:214
  670.7 46.8 %all-to-all-done.3 = bf16[32,40,2048]{2,1,0:T(8,128)(2,1)} async-done(((bf16[32,40,2048]{2,1,0:T(8,128)(2,1)}), bf16[32,40,2048]{2,1,0:T(8,128)(2,1)}, u32[]{:S(2)}, u32[]{:S(2)}) %all-to-all-start.3) | async-done | bytes 5242912 | tf_op jit(solution)/shard_map/all_to_all | solution.py:246
  717.5 12.0 gather_fusion.1
  767.1 13.0 %collective-permute-done.1 = bf16[128,2,2048]{2,0,1:T(8,128)(2,1)} collective-permute-done((bf16[128,2,2048]{2,0,1:T(8,128)(2,1)}, bf16[128,2,2048]{2,0,1:T(8,128)(2,1)}, u32[]{:S(2)}, u32[]{:S(2)}) %collective-permute-start.1) | collective-permute-done | bytes 1048608 | tf_op jit(solution)/shard_map/ppermute | solution.py:71
  799.6 14.3 %convolution_convert_fusion = bf16[4,2048,2048]{2,1,0:T(8,128)(2,1)} fusion(bf16[1,128,2048]{2,1,0:T(8,128)(2,1)S(1)} %copy-done.26, bf16[1,128,2048]{2,1,0:T(8,128)(2,1)S(1)} %copy-done.2, bf16[1,128,2048]{2,1,0:T(8,128)(2,1)S(1)} %copy-done.25, bf16[3,128,2048]{2,1,0:T(8,128)(2,1)S(1)} %maximum_bitcast_fusion.3), kind=kOutput, calls=%fused_computation.8 | convolution fusion | flops 4315938816 | bytes 36700160 | tf_op jit(solution)/shard_map/sta,stb->sab/dot_general | solution.py:331
  815.6 18.4 %fusion.80 = (f32[2048]{0:T(1024)S(1)}, f32[128]{0:T(128)S(1)}, f32[128,2048]{1,0:T(8,128)}) fusion(bf16[1,128,2048]{2,1,0:T(8,128)(2,1)S(1)} %copy-done.15, f32[128]{0:T(128)S(1)} %copy-done.62, f32[2048]{0:T(1024)S(1)} %copy-done.51, bf16[2048,4,2048]{2,0,1:T(8,128)(2,1)} %all-gather.2.cloned.1.call-done, bf16[128,1,2048]{2,0,1:T(8,128)(2,1)} %slice.230, ...), kind=kOutput, calls=%fused_computation.116 | convolution fusion | flops 4299945984 | bytes 36717576 | tf_op jit(solution)/shard_map/dot_general | solution.py:312
  852.0 15.6 %collective-permute-start.4 = (f32[73728]{0:T(1024)S(1)}, f32[73728]{0:T(1024)S(1)}, u32[]{:S(2)}, u32[]{:S(2)}) collective-permute-start(f32[73728]{0:T(1024)S(1)} %add.208), channel_id=1, source_target_pairs={{0,4},{1,5},{2,6},{3,7},{4,0},{5,1},{6,2},{7,3},{8,12},{9,13},{10,... | collective-permute-start | bytes 884744 | tf_op jit(solution)/shard_map/ppermute | solution.py:98
  909.0 14.1 %collective-permute-start.8 = (f32[73728]{0:T(1024)S(1)}, f32[73728]{0:T(1024)S(1)}, u32[]{:S(2)}, u32[]{:S(2)}) collective-permute-start(f32[73728]{0:T(1024)S(1)} %add.212), channel_id=1, source_target_pairs={{0,64},{1,65},{2,66},{3,67},{4,68},{5,69},{6,70},{7,71},{8,72},{9,... | collective-permute-start | bytes 884744 | tf_op jit(solution)/shard_map/ppermute | solution.py:98
  929.3 206.1 %all-reduce.2.cloned.1.call-done = bf16[4,2048,2048]{2,1,0:T(8,128)(2,1)} async-done(((bf16[4,2048,2048]{2,1,0:T(8,128)(2,1)}), bf16[4,2048,2048]{2,1,0:T(8,128)(2,1)}) %all-reduce.2.cloned.1.call-update) | async-done | bytes 33554448 | tf_op jit(solution)/shard_map/psum | solution.py:332
  1137.8 55.3 %reduce-scatter.7.cloned.1.call-done = bf16[2,512,1024]{1,2,0:T(8,128)(2,1)} async-done(((bf16[2,1024,1024]{1,2,0:T(8,128)(2,1)}), bf16[2,512,1024]{1,2,0:T(8,128)(2,1)}) %reduce-scatter.7.cloned.1.call-update) | async-done | bytes 2097168 | tf_op jit(solution)/shard_map/reduce_scatter | solution.py:324
  (279 shorter events, 232.8 us)
Async XLA Ops:
  7.2 366.5 %copy-start = (bf16[2048,32]{0,1:T(8,128)(2,1)S(1)}, bf16[2048,32]{0,1:T(8,128)(2,1)}, u32[]{:S(2)}) copy-start(bf16[2048,32]{0,1:T(8,128)(2,1)} %param.23) | copy-start | bytes 393220
  7.2 243.4 %all-gather.2.cloned.1.call-start = ((), (), s32[]{:S(2)}) async-start(), calls=%async_computation.8 | async-start | bytes 33816576 | tf_op jit(solution)/shard_map/all_gather | solution.py:137
  10.9 282.3 %copy-start.61 = (f32[128]{0:T(128)}, f32[128]{0:T(128)S(1)}, u32[]{:S(2)}) copy-start(f32[128]{0:T(128)S(1)} %add_rsqrt_fusion.3) | copy-start | bytes 1540
  11.9 301.2 %copy-start.38 = (f32[128,64]{1,0:T(8,128)}, f32[128,64]{1,0:T(8,128)S(1)}, u32[]{:S(2)}) copy-start(f32[128,64]{1,0:T(8,128)S(1)} %get-tuple-element.104) | copy-start | bytes 98308
  13.1 280.1 %copy-start.1 = (bf16[1,128,2048]{2,1,0:T(8,128)(2,1)}, bf16[1,128,2048]{2,1,0:T(8,128)(2,1)S(1)}, u32[]{:S(2)}) copy-start(bf16[1,128,2048]{2,1,0:T(8,128)(2,1)S(1)} %fusion.83) | copy-start | bytes 1572868
  315.8 23.9 %collective-permute-start = (bf16[128,2,2048]{2,0,1:T(8,128)(2,1)}, bf16[128,2,2048]{2,0,1:T(8,128)(2,1)S(1)}, u32[]{:S(2)}, u32[]{:S(2)}) collective-permute-start(bf16[128,2,2048]{2,0,1:T(8,128)(2,1)} %pad_maximum_fusion.2), channel_id=1, source_target_pairs={{0,32},{32,0},{1,33},{33,1},{2,34},{34,2},{3,35},{35,3},{4,36},{36... | collective-permute-start | bytes 3145736 | tf_op jit(solution)/shard_map/ppermute | solution.py:71
  366.3 74.2 %all-to-all-start = ((bf16[32,40,2048]{2,1,0:T(8,128)(2,1)}), bf16[32,40,2048]{2,1,0:T(8,128)(2,1)}, u32[]{:S(2)}, u32[]{:S(2)}) async-start(bf16[32,40,2048]{2,1,0:T(8,128)(2,1)} %bitcast.277), calls=%async_computation | async-start | bytes 10485760 | tf_op jit(solution)/shard_map/all_to_all | solution.py:195
  440.5 73.1 %all-to-all-start.2 = ((bf16[32,40,2048]{2,1,0:T(8,128)(2,1)}), bf16[32,40,2048]{2,1,0:T(8,128)(2,1)}, u32[]{:S(2)}, u32[]{:S(2)}) async-start(bf16[32,40,2048]{2,1,0:T(8,128)(2,1)} %bitcast.278), calls=%async_computation.2 | async-start | bytes 10485760 | tf_op jit(solution)/shard_map/all_to_all | solution.py:223
  447.1 319.9 %reduce-scatter.9.cloned.1.call-start = ((), (), s32[]{:S(2)}) async-start(), calls=%async_computation.12 | async-start | bytes 6291456 | tf_op jit(solution)/shard_map/reduce_scatter | solution.py:323
  523.8 290.3 %reduce-scatter.5.cloned.1.call-start = ((), (), s32[]{:S(2)}) async-start(), calls=%async_computation.10 | async-start | bytes 12582912 | tf_op jit(solution)/shard_map/reduce_scatter | solution.py:323
  565.7 74.2 %all-to-all-start.1 = ((bf16[32,40,2048]{2,1,0:T(8,128)(2,1)}), bf16[32,40,2048]{2,1,0:T(8,128)(2,1)}, u32[]{:S(2)}, u32[]{:S(2)}) async-start(bf16[32,40,2048]{2,1,0:T(8,128)(2,1)} %bitcast.284), calls=%async_computation.1 | async-start | bytes 10485760 | tf_op jit(solution)/shard_map/all_to_all | solution.py:211
  639.9 77.6 %all-to-all-start.3 = ((bf16[32,40,2048]{2,1,0:T(8,128)(2,1)}), bf16[32,40,2048]{2,1,0:T(8,128)(2,1)}, u32[]{:S(2)}, u32[]{:S(2)}) async-start(bf16[32,40,2048]{2,1,0:T(8,128)(2,1)} %bitcast.283), calls=%async_computation.3 | async-start | bytes 10485760 | tf_op jit(solution)/shard_map/all_to_all | solution.py:246
  651.1 275.3 %reduce-scatter.11.cloned.1.call-start = ((), (), s32[]{:S(2)}) async-start(), calls=%async_computation.13 | async-start | bytes 3145728 | tf_op jit(solution)/shard_map/reduce_scatter | solution.py:324
  761.4 18.6 %collective-permute-start.1 = (bf16[128,2,2048]{2,0,1:T(8,128)(2,1)}, bf16[128,2,2048]{2,0,1:T(8,128)(2,1)}, u32[]{:S(2)}, u32[]{:S(2)}) collective-permute-start(bf16[128,2,2048]{2,0,1:T(8,128)(2,1)} %select_convert_fusion), channel_id=1, source_target_pairs={{0,32},{32,0},{1,33},{33,1},{2,34},{34,2},{3,35},{35,3},{4,36},{36... | collective-permute-start | bytes 3145736 | tf_op jit(solution)/shard_map/ppermute | solution.py:71
  767.0 368.4 %all-reduce.2.cloned.1.call-start = ((), (), s32[]{:S(2)}) async-start(), calls=%async_computation.9 | async-start | bytes 67108864 | tf_op jit(solution)/shard_map/psum | solution.py:332
  813.9 379.2 %reduce-scatter.7.cloned.1.call-start = ((), (), s32[]{:S(2)}) async-start(), calls=%async_computation.11 | async-start | bytes 6291456 | tf_op jit(solution)/shard_map/reduce_scatter | solution.py:324
  834.0 89.1 %copy-start.37 = (f32[128,2048]{1,0:T(8,128)S(1)}, f32[128,2048]{1,0:T(8,128)}, u32[]{:S(2)}) copy-start(f32[128,2048]{1,0:T(8,128)} %get-tuple-element.110) | copy-start | bytes 3145732
  834.0 7.2 collective-permute-start.2
  841.2 10.7 collective-permute-start.3
  852.0 22.8 %collective-permute-start.4 = (f32[73728]{0:T(1024)S(1)}, f32[73728]{0:T(1024)S(1)}, u32[]{:S(2)}, u32[]{:S(2)}) collective-permute-start(f32[73728]{0:T(1024)S(1)} %add.208), channel_id=1, source_target_pairs={{0,4},{1,5},{2,6},{3,7},{4,0},{5,1},{6,2},{7,3},{8,12},{9,13},{10,... | collective-permute-start | bytes 884744 | tf_op jit(solution)/shard_map/ppermute | solution.py:98
  874.8 9.0 collective-permute-start.5
  883.9 14.0 %collective-permute-start.6 = (f32[73728]{0:T(1024)S(1)}, f32[73728]{0:T(1024)S(1)}, u32[]{:S(2)}, u32[]{:S(2)}) collective-permute-start(f32[73728]{0:T(1024)S(1)} %add.210), channel_id=1, source_target_pairs={{0,16},{1,17},{2,18},{3,19},{4,20},{5,21},{6,22},{7,23},{8,24},{9,... | collective-permute-start | bytes 884744 | tf_op jit(solution)/shard_map/ppermute | solution.py:98
  897.9 10.1 collective-permute-start.7
  909.0 15.4 %collective-permute-start.8 = (f32[73728]{0:T(1024)S(1)}, f32[73728]{0:T(1024)S(1)}, u32[]{:S(2)}, u32[]{:S(2)}) collective-permute-start(f32[73728]{0:T(1024)S(1)} %add.212), channel_id=1, source_target_pairs={{0,64},{1,65},{2,66},{3,67},{4,68},{5,69},{6,70},{7,71},{8,72},{9,... | collective-permute-start | bytes 884744 | tf_op jit(solution)/shard_map/ppermute | solution.py:98
  (60 other events, 387.7 us)
Sparse Core Ops, SparseCore 0:
  10.3 240.1 all-gather.1
  523.9 21.7 reduce-scatter.8
  556.0 26.1 reduce-scatter.4
  767.1 43.3 reduce-scatter.10
  816.8 318.5 all-reduce.1
  1137.8 55.2 reduce-scatter.6
where the time goes:
time: 1220 us; the launch traced here: 1210 us
  waiting for transfers between devices  763 us (63%)
  matrix products  165 us (14%)
  local copies, waits for them, and re-layouts  128 us (10%)
  starting transfers between devices  80.6 us (7%)
  other arithmetic  57.7 us (5%)
  between operations  15.5 us (1%)
    all_gather x1, waiting for transfers between devices, body(): lax.all_gather(jnp.concatenate([qkv_weight.transpose(1, 0, 2), out_weight...  237 us
    psum x1, waiting for transfers between devices, body(): summed = lax.psum(stacked.astype(bf16), all_axes)  206 us
    reduce_scatter x2, waiting for transfers between devices, scatter_over_copies(): lax.psum_scatter(values, 'context', scatter_dimension=1, tiled=True)  55.3 us
    all_to_all x1, waiting for transfers between devices, body(): lax.all_to_all(send.reshape(sources, local_experts * capacity, width), 'e...  49 us
    all_to_all x1, waiting for transfers between devices, body(): lax.all_to_all(source_major(grad_rows_in, sources, capacity), 'expert', s...  46.8 us
    all_to_all x1, waiting for transfers between devices, body(): lax.all_to_all(source_major(results, sources, capacity), 'expert', split_...  46.6 us
    ppermute x7, starting transfers between devices, butterfly_sum(): received = lax.ppermute(values, axes, partner)  44 us
    ppermute x7, waiting for transfers between devices, butterfly_sum(): received = lax.ppermute(values, axes, partner)  43.8 us
  transfers between devices with their start and end apart: 19, of which 15 were waited for; matrix products, arithmetic and copies ran while one was open for 19% of the time, Pallas kernels for 0%

commit v1 on v0

--- a/solution.py
+++ b/solution.py
@@ -134,11 +134,17 @@
     normed1, factor1 = rms_forward(x)
     attention_input = (normed1 * attn_gain).astype(bf16)
     all_axes = ("dp", "context", "expert")
-    weights_full = lax.all_gather(
-        jnp.concatenate([qkv_weight.transpose(1, 0, 2), out_weight[:, None, :]], axis=1),
-        all_axes,
+    weights_full = jnp.concatenate(
+        lax.all_to_all(
+            jnp.stack(
+                [jnp.concatenate([qkv_weight.transpose(1, 0, 2), out_weight[:, None, :]], axis=1)]
+                * lax.axis_size(all_axes)
+            ),
+            all_axes,
+            0,
+            0,
+        ),
         axis=0,
-        tiled=True,
     )
     out_full = weights_full[:, 3, :]
     projected_all = jnp.dot(

time: 1220 us -> 1710 us (1.40)
  waiting for transfers between devices: 763 us -> 1080 us
  local copies, waits for them, and re-layouts: 128 us -> 237 us
  starting transfers between devices: 80.6 us -> 143 us
    all_to_all x0 -> x1, waiting for transfers between devices: none -> 585 us  [body(): lax.all_to_all(jnp.stack([jnp.concatenate([qkv_weight.transpose(1, 0, 2),...]
    all_gather x1 -> x0, waiting for transfers between devices: 237 us -> none  [body(): lax.all_gather(jnp.concatenate([qkv_weight.transpose(1, 0, 2), out_weight...]
    all_to_all x0 -> x2, local copies, waits for them, and re-layouts: none -> 60.5 us  [body(): lax.all_to_all(jnp.stack([jnp.concatenate([qkv_weight.transpose(1, 0, 2),...]
    reduce_scatter x2, waiting for transfers between devices: 55.3 us -> 0.01 us  [scatter_over_copies(): lax.psum_scatter(values, 'context', scatter_dimension=1, tiled=True)]
    all_to_all x1, starting transfers between devices: 7.06 us -> 58.3 us  [body(): lax.all_to_all(send.reshape(sources, local_experts * capacity, width), 'e...]
    dot_general x0 -> x1, local copies, waits for them, and re-layouts: none -> 44.4 us  [body(): jnp.dot(attention_input, weights_full.reshape(width, 4 * heads_width), pr...]
    all_gather x1 -> x0, local copies, waits for them, and re-layouts: 42.7 us -> none  [body(): lax.all_gather(jnp.concatenate([qkv_weight.transpose(1, 0, 2), out_weight...]
    psum x1, waiting for transfers between devices: 206 us -> 244 us  [body(): summed = lax.psum(stacked.astype(bf16), all_axes)]
  transfers between devices with their start and end apart: 19 -> 19, of which waited for: 15 -> 13; matrix products, arithmetic and copies ran while one was open for 19% -> 15% of each run, Pallas kernels for 0% -> 0%
where the time goes in v1:
time: 1710 us; the launch traced here: 1700 us
  waiting for transfers between devices  1080 us (63%)
  local copies, waits for them, and re-layouts  237 us (14%)
  matrix products  163 us (10%)
  starting transfers between devices  143 us (8%)
  other arithmetic  58.5 us (3%)
    all_to_all x1, waiting for transfers between devices, body(): lax.all_to_all(jnp.stack([jnp.concatenate([qkv_weight.transpose(1, 0, 2),...  585 us
    psum x1, waiting for transfers between devices, body(): summed = lax.psum(stacked.astype(bf16), all_axes)  244 us
    all_to_all x2, local copies, waits for them, and re-layouts, body(): lax.all_to_all(jnp.stack([jnp.concatenate([qkv_weight.transpose(1, 0, 2),...  60.5 us
    all_to_all x1, starting transfers between devices, body(): lax.all_to_all(send.reshape(sources, local_experts * capacity, width), 'e...  58.3 us
    unnamed x155, local copies, waits for them, and re-layouts  53.1 us
    ppermute x7, waiting for transfers between devices, butterfly_sum(): received = lax.ppermute(values, axes, partner)  49.3 us
    all_to_all x1, waiting for transfers between devices, body(): lax.all_to_all(source_major(results, sources, capacity), 'expert', split_...  49 us
    all_to_all x1, waiting for transfers between devices, body(): lax.all_to_all(send.reshape(sources, local_experts * capacity, width), 'e...  47.9 us
  transfers between devices with their start and end apart: 19, of which 13 were waited for; matrix products, arithmetic and copies ran while one was open for 15% of the time, Pallas kernels for 0%

profile of v1, /device:TPU:1, one launch (start us, length us, event | category | flops | bytes accessed | tf_op | source)
XLA Modules:
  0.0 1700.5 jit_solution(8034296440464740312)
XLA Ops:
  20.1 12.0 all-to-all-start
  33.5 585.1 %all-to-all-done = bf16[128,16,4,2048]{3,1,2,0:T(8,128)(2,1)} async-done(((bf16[128,16,4,2048]{3,1,2,0:T(8,128)(2,1)}), bf16[128,16,4,2048]{3,1,2,0:T(8,128)(2,1)}, u32[]{:S(2)}, u32[]{:S(2)}) %all-to-all-start) | async-done | bytes 33554464 | tf_op jit(solution)/shard_map/all_to_all | solution.py:138
  618.6 37.6 %copy.149 = bf16[128,16,4,2048]{3,2,1,0:T(4,128)(2,1)} copy(bf16[128,16,4,2048]{3,1,2,0:T(8,128)(2,1)} %all-to-all-done) | data formatting | bytes 67108864 | tf_op jit(solution)/shard_map/all_to_all | solution.py:138
  656.2 30.1 %copy.197 = bf16[256,8,4,2048]{3,1,2,0:T(8,128)(2,1)} copy(bf16[256,8,4,2048]{3,2,1,0:T(4,128)(2,1)} %bitcast.279) | data formatting | bytes 67108864
  686.2 44.4 %copy.150 = bf16[8192,2048]{1,0:T(8,128)(2,1)} copy(bf16[8192,2048]{0,1:T(8,128)(2,1)} %bitcast.276) | data formatting | bytes 67108864 | tf_op jit(solution)/shard_map/dot_general | solution.py:150
  730.7 17.2 %convolution_bitcast_fusion = f32[3,128,2048]{2,1,0:T(8,128)S(1)} fusion(bf16[4,2048,2048]{2,1,0:T(8,128)(2,1)} %bitcast.278, bf16[1,128,2048]{2,1,0:T(8,128)(2,1)S(1)} %fusion.72), kind=kOutput, calls=%fused_computation.52 | convolution fusion | flops 3221225472 | bytes 37224448 | tf_op jit(solution)/shard_map/slice | solution.py:155
  753.2 16.4 collective-permute-start
  770.6 23.0 %copy.156 = bf16[128,16,4,2048]{3,1,0,2:T(8,128)(2,1)} copy(bf16[128,16,4,2048]{3,1,2,0:T(8,128)(2,1)} %all-to-all-done) | data formatting | bytes 67108864 | tf_op jit(solution)/shard_map/all_to_all | solution.py:138
  823.8 58.3 %all-to-all-start.1 = ((bf16[32,40,2048]{2,1,0:T(8,128)(2,1)}), bf16[32,40,2048]{2,1,0:T(8,128)(2,1)}, u32[]{:S(2)}, u32[]{:S(2)}) async-start(bf16[32,40,2048]{2,1,0:T(8,128)(2,1)} %bitcast.282), calls=%async_computation.1 | async-start | bytes 10485760 | tf_op jit(solution)/shard_map/all_to_all | solution.py:201
  900.4 47.9 %all-to-all-done.1 = bf16[32,40,2048]{2,1,0:T(8,128)(2,1)} async-done(((bf16[32,40,2048]{2,1,0:T(8,128)(2,1)}), bf16[32,40,2048]{2,1,0:T(8,128)(2,1)}, u32[]{:S(2)}, u32[]{:S(2)}) %all-to-all-start.1) | async-done | bytes 5242912 | tf_op jit(solution)/shard_map/all_to_all | solution.py:201
  958.4 16.8 fusion.9
  981.9 42.4 %all-to-all-done.3 = bf16[32,40,2048]{2,1,0:T(8,128)(2,1)} async-done(((bf16[32,40,2048]{2,1,0:T(8,128)(2,1)}), bf16[32,40,2048]{2,1,0:T(8,128)(2,1)}, u32[]{:S(2)}, u32[]{:S(2)}) %all-to-all-start.3) | async-done | bytes 5242912 | tf_op jit(solution)/shard_map/all_to_all | solution.py:229
  1034.7 13.1 fusion.36
  1050.6 16.0 convert_bitcast_fusion
  1086.0 17.3 %bitcast_convert_fusion = bf16[1280,2048]{1,0:T(8,128)(2,1)} fusion(bf16[1,2,2048,1024]{3,2,1,0:T(8,128)(2,1)} %param.24, bf16[1,1,1280,1024]{3,2,1,0:T(8,128)(2,1)} %copy-done.70, bf16[1,1,1280,1024]{3,2,1,0:T(8,128)(2,1)} %copy-done.69), kind=kOutput, calls=%fused_computation.9 | convolution fusion | flops 10742661120 | bytes 18874368 | tf_op jit(solution)/shard_map/lkrh,lkdh->lrd/dot_general | solution.py:249
  1103.3 49.0 %all-to-all-done.2 = bf16[32,40,2048]{2,1,0:T(8,128)(2,1)} async-done(((bf16[32,40,2048]{2,1,0:T(8,128)(2,1)}), bf16[32,40,2048]{2,1,0:T(8,128)(2,1)}, u32[]{:S(2)}, u32[]{:S(2)}) %all-to-all-start.2) | async-done | bytes 5242912 | tf_op jit(solution)/shard_map/all_to_all | solution.py:217
  1164.5 12.4 gather_fusion
  1181.9 46.2 %all-to-all-done.4 = bf16[32,40,2048]{2,1,0:T(8,128)(2,1)} async-done(((bf16[32,40,2048]{2,1,0:T(8,128)(2,1)}), bf16[32,40,2048]{2,1,0:T(8,128)(2,1)}, u32[]{:S(2)}, u32[]{:S(2)}) %all-to-all-start.4) | async-done | bytes 5242912 | tf_op jit(solution)/shard_map/all_to_all | solution.py:252
  1228.1 12.0 gather_fusion.1
  1276.6 17.9 %collective-permute-done.1 = bf16[128,2,2048]{2,0,1:T(8,128)(2,1)} collective-permute-done((bf16[128,2,2048]{2,0,1:T(8,128)(2,1)}, bf16[128,2,2048]{2,0,1:T(8,128)(2,1)}, u32[]{:S(2)}, u32[]{:S(2)}) %collective-permute-start.1) | collective-permute-done | bytes 1048608 | tf_op jit(solution)/shard_map/ppermute | solution.py:71
  1314.6 14.3 convolution_convert_fusion
  1336.2 17.9 %fusion.69 = (f32[2048]{0:T(1024)S(1)}, f32[128]{0:T(128)}, f32[128,2048]{1,0:T(8,128)}) fusion(bf16[1,128,2048]{2,1,0:T(8,128)(2,1)S(1)} %copy-done.13, f32[128]{0:T(128)S(1)} %copy-done.64, f32[2048]{0:T(1024)S(1)} %copy-done.52, bf16[128,8192]{0,1:T(8,128)(2,1)S(1)} %bitcast.284, bf16[2048,8192]{1,0:T(8,128)(2,1)} %bitcast.277), kind=kOutput, calls=%fused_computation.108 | convolution fusion | flops 4296800256 | bytes 37241856 | tf_op jit(solution)/shard_map/dot_general | solution.py:318
  1354.3 13.1 collective-permute-done.2
  1437.1 244.2 %all-reduce.2.cloned.1.call-done = bf16[4,2048,2048]{2,1,0:T(8,128)(2,1)} async-done(((bf16[4,2048,2048]{2,1,0:T(8,128)(2,1)}), bf16[4,2048,2048]{2,1,0:T(8,128)(2,1)}) %all-reduce.2.cloned.1.call-update) | async-done | bytes 33554448 | tf_op jit(solution)/shard_map/psum | solution.py:338
  (296 shorter events, 279.1 us)
Async XLA Ops:
  8.0 874.4 %copy-start = (bf16[2048,32]{0,1:T(8,128)(2,1)S(1)}, bf16[2048,32]{0,1:T(8,128)(2,1)}, u32[]{:S(2)}) copy-start(bf16[2048,32]{0,1:T(8,128)(2,1)} %param.23) | copy-start | bytes 393220
  20.1 598.5 %all-to-all-start = ((bf16[128,16,4,2048]{3,1,2,0:T(8,128)(2,1)}), bf16[128,16,4,2048]{3,1,2,0:T(8,128)(2,1)}, u32[]{:S(2)}, u32[]{:S(2)}) async-start(bf16[128,16,4,2048]{3,1,2,0:T(8,128)(2,1)} %stack.21), calls=%async_computation | async-start | bytes 67108864 | tf_op jit(solution)/shard_map/all_to_all | solution.py:138
  32.4 623.8 %copy-start.63 = (f32[128]{0:T(128)}, f32[128]{0:T(128)S(1)}, u32[]{:S(2)}) copy-start(f32[128]{0:T(128)S(1)} %add_rsqrt_fusion.3) | copy-start | bytes 1540
  33.3 717.1 %copy-start.38 = (f32[128,64]{1,0:T(8,128)}, f32[128,64]{1,0:T(8,128)S(1)}, u32[]{:S(2)}) copy-start(f32[128,64]{1,0:T(8,128)S(1)} %get-tuple-element.115) | copy-start | bytes 98308
  33.5 697.1 %copy-start.1 = (bf16[1,128,2048]{2,1,0:T(8,128)(2,1)}, bf16[1,128,2048]{2,1,0:T(8,128)(2,1)S(1)}, u32[]{:S(2)}) copy-start(bf16[1,128,2048]{2,1,0:T(8,128)(2,1)S(1)} %fusion.72) | copy-start | bytes 1572868
  753.2 40.4 %collective-permute-start = (bf16[128,2,2048]{2,0,1:T(8,128)(2,1)}, bf16[128,2,2048]{2,0,1:T(8,128)(2,1)}, u32[]{:S(2)}, u32[]{:S(2)}) collective-permute-start(bf16[128,2,2048]{2,0,1:T(8,128)(2,1)} %pad_maximum_fusion.2), channel_id=1, source_target_pairs={{0,32},{32,0},{1,33},{33,1},{2,34},{34,2},{3,35},{35,3},{4,36},{36... | collective-permute-start | bytes 3145736 | tf_op jit(solution)/shard_map/ppermute | solution.py:71
  823.8 124.6 %all-to-all-start.1 = ((bf16[32,40,2048]{2,1,0:T(8,128)(2,1)}), bf16[32,40,2048]{2,1,0:T(8,128)(2,1)}, u32[]{:S(2)}, u32[]{:S(2)}) async-start(bf16[32,40,2048]{2,1,0:T(8,128)(2,1)} %bitcast.282), calls=%async_computation.1 | async-start | bytes 10485760 | tf_op jit(solution)/shard_map/all_to_all | solution.py:201
  948.3 76.0 %all-to-all-start.3 = ((bf16[32,40,2048]{2,1,0:T(8,128)(2,1)}), bf16[32,40,2048]{2,1,0:T(8,128)(2,1)}, u32[]{:S(2)}, u32[]{:S(2)}) async-start(bf16[32,40,2048]{2,1,0:T(8,128)(2,1)} %bitcast.283), calls=%async_computation.3 | async-start | bytes 10485760 | tf_op jit(solution)/shard_map/all_to_all | solution.py:229
  957.9 318.6 %reduce-scatter.9.cloned.1.call-start = ((), (), s32[]{:S(2)}) async-start(), calls=%async_computation.12 | async-start | bytes 6291456 | tf_op jit(solution)/shard_map/reduce_scatter | solution.py:329
  1034.4 294.8 %reduce-scatter.5.cloned.1.call-start = ((), (), s32[]{:S(2)}) async-start(), calls=%async_computation.10 | async-start | bytes 12582912 | tf_op jit(solution)/shard_map/reduce_scatter | solution.py:329
  1076.5 75.8 %all-to-all-start.2 = ((bf16[32,40,2048]{2,1,0:T(8,128)(2,1)}), bf16[32,40,2048]{2,1,0:T(8,128)(2,1)}, u32[]{:S(2)}, u32[]{:S(2)}) async-start(bf16[32,40,2048]{2,1,0:T(8,128)(2,1)} %bitcast.290), calls=%async_computation.2 | async-start | bytes 10485760 | tf_op jit(solution)/shard_map/all_to_all | solution.py:217
  1152.3 75.8 %all-to-all-start.4 = ((bf16[32,40,2048]{2,1,0:T(8,128)(2,1)}), bf16[32,40,2048]{2,1,0:T(8,128)(2,1)}, u32[]{:S(2)}, u32[]{:S(2)}) async-start(bf16[32,40,2048]{2,1,0:T(8,128)(2,1)} %bitcast.289), calls=%async_computation.4 | async-start | bytes 10485760 | tf_op jit(solution)/shard_map/all_to_all | solution.py:252
  1161.9 272.2 %reduce-scatter.11.cloned.1.call-start = ((), (), s32[]{:S(2)}) async-start(), calls=%async_computation.13 | async-start | bytes 3145728 | tf_op jit(solution)/shard_map/reduce_scatter | solution.py:330
  1271.8 22.7 %collective-permute-start.1 = (bf16[128,2,2048]{2,0,1:T(8,128)(2,1)}, bf16[128,2,2048]{2,0,1:T(8,128)(2,1)}, u32[]{:S(2)}, u32[]{:S(2)}) collective-permute-start(bf16[128,2,2048]{2,0,1:T(8,128)(2,1)} %select_convert_fusion), channel_id=1, source_target_pairs={{0,32},{32,0},{1,33},{33,1},{2,34},{34,2},{3,35},{35,3},{4,36},{36... | collective-permute-start | bytes 3145736 | tf_op jit(solution)/shard_map/ppermute | solution.py:71
  1276.5 404.7 %all-reduce.2.cloned.1.call-start = ((), (), s32[]{:S(2)}) async-start(), calls=%async_computation.9 | async-start | bytes 67108864 | tf_op jit(solution)/shard_map/psum | solution.py:338
  1329.0 354.7 %reduce-scatter.7.cloned.1.call-start = ((), (), s32[]{:S(2)}) async-start(), calls=%async_computation.11 | async-start | bytes 6291456 | tf_op jit(solution)/shard_map/reduce_scatter | solution.py:330
  1354.2 76.1 %copy-start.30 = (f32[128,2048]{1,0:T(8,128)S(1)}, f32[128,2048]{1,0:T(8,128)}, u32[]{:S(2)}) copy-start(f32[128,2048]{1,0:T(8,128)} %copy-done.29) | copy-start | bytes 3145732
  1354.2 13.2 collective-permute-start.2
  1367.5 13.8 collective-permute-start.3
  1381.4 13.9 collective-permute-start.4
  1395.4 7.3 collective-permute-start.5
  1402.7 8.2 collective-permute-start.6
  1410.9 9.1 collective-permute-start.7
  1420.1 12.1 collective-permute-start.8
  (66 other events, 689.8 us)
Sparse Core Ops, SparseCore 0:
  1034.6 18.2 reduce-scatter.8
  1066.8 22.3 reduce-scatter.4
  1276.7 44.3 reduce-scatter.10
  1332.0 76.5 reduce-scatter.6
Sparse Core Ops, SparseCore 1:
  1329.1 352.2 all-reduce.1
